TPU v7x, 32 devices: a whole 2x2x4 slice. The times are simulated.
32 devices in a mesh: dp: 16 (over z, y, x), seq: 2 (over core).
Axes of the slice: x: 2, y: 2, z: 4, core: 2. Of those that a mesh axis runs over, the one named last changes fastest.
Arguments:
- tokens: bfloat16 [48, 512, 768], P('dp', 'seq'), may hold values from -6 to 6
- prev_logits: bfloat16 [48, 12, 512, 512], P('dp', None, 'seq'), may hold values from -6 to 6
- segment_ids: int32 [48, 512], P('dp'), may hold values from 0 to 5, never falling along the last dimension, each value on 1 to 192 neighbouring positions
- out_cotangent: bfloat16 [48, 512, 768], P('dp', 'seq'), may hold values from -6 to 6
- logit_cotangent: bfloat16 [48, 12, 512, 512], P('dp', None, 'seq'), may hold values from -0.59765625 to 0.59765625
- querymap: bfloat16 [768, 768], P(('dp', 'seq')), may hold values from -0.21875 to 0.21875
- querybias: bfloat16 [768], P(('dp', 'seq')), may hold values from -3 to 3
- keymap: bfloat16 [768, 768], P(('dp', 'seq')), may hold values from -0.21875 to 0.21875
- valuemap: bfloat16 [768, 768], P(('dp', 'seq')), may hold values from -0.21875 to 0.21875
- valuebias: bfloat16 [768], P(('dp', 'seq')), may hold values from -3 to 3
- mixmap: bfloat16 [768, 768], P(('dp', 'seq')), may hold values from -1.75 to 1.75
- mixbias: bfloat16 [768], P(('dp', 'seq')), may hold values from -3 to 3
- normgain: bfloat16 [768], P(('dp', 'seq')), may hold values from 0.5 to 1.5
- normbias: bfloat16 [768], P(('dp', 'seq')), may hold values from -3 to 3
- expandmap: bfloat16 [768, 3072], P(('dp', 'seq')), may hold values from -0.21875 to 0.21875
- expandbias: bfloat16 [3072], P(('dp', 'seq')), may hold values from -3 to 3
- shrinkmap: bfloat16 [3072, 768], P(('dp', 'seq')), may hold values from -0.109375 to 0.109375
- shrinkbias: bfloat16 [768], P(('dp', 'seq')), may hold values from -3 to 3
- outgain: bfloat16 [768], P(('dp', 'seq')), may hold values from 0.5 to 1.5
- outbias: bfloat16 [768], P(('dp', 'seq')), may hold values from -3 to 3
Outputs:
- layer_out: bfloat16 [48, 512, 768], P('dp', 'seq')
- raw_logits: bfloat16 [48, 12, 512, 512], P('dp', None, 'seq')
- tokens_grad: bfloat16 [48, 512, 768], P('dp', 'seq')
- logits_grad: bfloat16 [48, 12, 512, 512], P('dp', None, 'seq')
- querymap_grad: float32 [768, 768], P(('dp', 'seq'))
- querybias_grad: float32 [768], P(('dp', 'seq'))
- keymap_grad: float32 [768, 768], P(('dp', 'seq'))
- valuemap_grad: float32 [768, 768], P(('dp', 'seq'))
- valuebias_grad: float32 [768], P(('dp', 'seq'))
- mixmap_grad: float32 [768, 768], P(('dp', 'seq'))
- mixbias_grad: float32 [768], P(('dp', 'seq'))
- normgain_grad: float32 [768], P(('dp', 'seq'))
- normbias_grad: float32 [768], P(('dp', 'seq'))
- expandmap_grad: float32 [768, 3072], P(('dp', 'seq'))
- expandbias_grad: float32 [3072], P(('dp', 'seq'))
- shrinkmap_grad: float32 [3072, 768], P(('dp', 'seq'))
- shrinkbias_grad: float32 [768], P(('dp', 'seq'))
- outgain_grad: float32 [768], P(('dp', 'seq'))
- outbias_grad: float32 [768], P(('dp', 'seq'))
Inputs may be any that keep to these rules, and one draw needn't show every extreme that they name: `segment_ids`: along each row the ids never fall; each id covers 1 to 192 slots and in each row one covers exactly that many.
All inputs are finite; a program needn't handle non-finite values.
Results may differ from a plain program's by a relative error of at most 0.014.
Values may be sent and summed in bfloat16 or wider, within the bound.
A program may use at most 192 MiB of HBM per device.

v0:
```python
from functools import partial
import jax
import jax.numpy as jnp
from jax import lax
from jax.sharding import PartitionSpec as P

H = 12
HD = 64
norm_eps = 1e-06
mask_fill = -1e30


def matmul(left_side, right_side):
    return jnp.dot(left_side, right_side, preferred_element_type=jnp.float32)


def rows_product(left_side, right_side):
    return lax.dot_general(
        left_side, right_side, (((0,), (0,)), ((), ())), preferred_element_type=jnp.float32
    )


def cols_product(left_side, right_side):
    return lax.dot_general(
        left_side, right_side, (((1,), (1,)), ((), ())), preferred_element_type=jnp.float32
    )


def column_sum(matrix):
    return jnp.sum(matrix.astype(jnp.float32), 0)


def normalize(hidden):
    center = hidden - jnp.mean(hidden, -1, keepdims=True)
    scaled = lax.rsqrt(jnp.mean(center * center, -1, keepdims=True) + norm_eps)
    return (center * scaled, scaled)


def norm_back(upstream, unit_rows, scaled, gain_row):
    pulled = upstream * gain_row
    return scaled * (
        pulled
        - jnp.mean(pulled, -1, keepdims=True)
        - unit_rows * jnp.mean(pulled * unit_rows, -1, keepdims=True)
    )


def forward(shards, tokens, prev_logits, same_segment):
    (
        querymap,
        querybias,
        keymap,
        valuemap,
        valuebias,
        mixmap,
        mixbias,
        normgain,
        normbias,
        expandmap,
        expandbias,
        shrinkmap,
        shrinkbias,
        outgain,
        outbias,
    ) = shards
    weights = (
        lax.all_gather(querymap, ("dp", "seq"), axis=0, tiled=True),
        lax.all_gather(querybias, ("dp", "seq"), axis=0, tiled=True),
        lax.all_gather(keymap, ("dp", "seq"), axis=0, tiled=True),
        lax.all_gather(valuemap, ("dp", "seq"), axis=0, tiled=True),
        lax.all_gather(valuebias, ("dp", "seq"), axis=0, tiled=True),
        lax.all_gather(mixmap, ("dp", "seq"), axis=0, tiled=True),
        lax.all_gather(mixbias, ("dp", "seq"), axis=0, tiled=True),
        lax.all_gather(normgain, ("dp", "seq"), axis=0, tiled=True),
        lax.all_gather(normbias, ("dp", "seq"), axis=0, tiled=True),
        lax.all_gather(expandmap, ("dp", "seq"), axis=0, tiled=True),
        lax.all_gather(expandbias, ("dp", "seq"), axis=0, tiled=True),
        lax.all_gather(shrinkmap, ("dp", "seq"), axis=0, tiled=True),
        lax.all_gather(shrinkbias, ("dp", "seq"), axis=0, tiled=True),
        lax.all_gather(outgain, ("dp", "seq"), axis=0, tiled=True),
        lax.all_gather(outbias, ("dp", "seq"), axis=0, tiled=True),
    )
    (
        querymap,
        querybias,
        keymap,
        valuemap,
        valuebias,
        mixmap,
        mixbias,
        normgain,
        normbias,
        expandmap,
        expandbias,
        shrinkmap,
        shrinkbias,
        outgain,
        outbias,
    ) = weights
    seqrows, qlength, width = tokens.shape
    klength = prev_logits.shape[3]
    factor = HD ** (-0.5)
    token_rows = tokens.reshape(seqrows * qlength, width)
    queries = (matmul(token_rows, querymap) + querybias.astype(jnp.float32)).astype(jnp.bfloat16)
    keys_local = matmul(token_rows, keymap).astype(jnp.bfloat16)
    values_local = (matmul(token_rows, valuemap) + valuebias.astype(jnp.float32)).astype(
        jnp.bfloat16
    )
    keys_all, values_all = (
        lax.all_gather(keys_local.reshape(seqrows, qlength, width), "seq", axis=1, tiled=True),
        lax.all_gather(values_local.reshape(seqrows, qlength, width), "seq", axis=1, tiled=True),
    )
    query_heads = queries.reshape(seqrows, qlength, H, HD)
    key_heads = keys_all.reshape(seqrows, klength, H, HD)
    value_heads = values_all.reshape(seqrows, klength, H, HD)

    def attend(operands):
        query_one, key_one, value_one, prior_one, same_one = operands
        scores = jnp.einsum("qhe,khe->hqk", query_one, key_one, preferred_element_type=jnp.float32)
        logits = prior_one.astype(jnp.float32) + scores * factor
        masked = jnp.where(same_one, logits, mask_fill)
        row_peak = jnp.max(masked, -1, keepdims=True)
        exponent = jnp.exp(masked - row_peak)
        row_total = jnp.sum(exponent, -1, keepdims=True)
        attention = (exponent / row_total).astype(jnp.bfloat16)
        context = jnp.einsum(
            "hqk,khe->qhe", attention, value_one, preferred_element_type=jnp.float32
        )
        return (
            logits.astype(jnp.bfloat16),
            context.astype(jnp.bfloat16),
            row_peak + jnp.log(row_total),
        )

    raw_logits, context, log_total = lax.map(
        attend, (query_heads, key_heads, value_heads, prev_logits, same_segment)
    )
    context = context.reshape(seqrows * qlength, width)
    attended = matmul(context, mixmap) + mixbias.astype(jnp.float32)
    unit_first, scale_first = normalize(token_rows.astype(jnp.float32) + attended)
    normed = (unit_first * normgain.astype(jnp.float32) + normbias.astype(jnp.float32)).astype(
        jnp.bfloat16
    )
    inner_pre = matmul(normed, expandmap) + expandbias.astype(jnp.float32)
    active = jax.nn.gelu(inner_pre, approximate=False).astype(jnp.bfloat16)
    second = normed.astype(jnp.float32) + (
        matmul(active, shrinkmap) + shrinkbias.astype(jnp.float32)
    )
    unit_second, scale_second = normalize(second)
    layer_out = unit_second * outgain.astype(jnp.float32) + outbias.astype(jnp.float32)
    return (
        weights,
        queries,
        key_heads,
        value_heads,
        log_total,
        context,
        unit_first,
        scale_first,
        normed,
        inner_pre,
        active,
        unit_second,
        scale_second,
        raw_logits,
        layer_out,
    )


def body(
    tokens,
    prev_logits,
    segment_ids,
    out_cotangent,
    logit_cotangent,
    querymap,
    querybias,
    keymap,
    valuemap,
    valuebias,
    mixmap,
    mixbias,
    normgain,
    normbias,
    expandmap,
    expandbias,
    shrinkmap,
    shrinkbias,
    outgain,
    outbias,
):
    shards = (
        querymap,
        querybias,
        keymap,
        valuemap,
        valuebias,
        mixmap,
        mixbias,
        normgain,
        normbias,
        expandmap,
        expandbias,
        shrinkmap,
        shrinkbias,
        outgain,
        outbias,
    )
    seqrows, qlength, width = tokens.shape
    klength = segment_ids.shape[1]
    factor = HD ** (-0.5)
    own_segment = lax.dynamic_slice_in_dim(segment_ids, lax.axis_index("seq") * qlength, qlength, 1)
    same_segment = (own_segment[:, :, None] == segment_ids[:, None, :])[:, None]
    first_pass = forward(shards, tokens, prev_logits, same_segment)
    fenced = lax.optimization_barrier((shards, tokens, prev_logits, same_segment, first_pass[14]))
    state = forward(fenced[0], fenced[1], fenced[2], fenced[3])
    (
        weights,
        queries,
        key_heads,
        value_heads,
        log_total,
        context,
        unit_first,
        scale_first,
        normed,
        inner_pre,
        active,
        unit_second,
        scale_second,
        unused_logits,
        unused_output,
    ) = state
    raw_logits = first_pass[13]
    layer_out = first_pass[14]
    (
        querymap,
        querybias,
        keymap,
        valuemap,
        valuebias,
        mixmap,
        mixbias,
        normgain,
        normbias,
        expandmap,
        expandbias,
        shrinkmap,
        shrinkbias,
        outgain,
        outbias,
    ) = weights
    token_rows = tokens.reshape(seqrows * qlength, width)
    upstream = out_cotangent.reshape(seqrows * qlength, width).astype(jnp.float32)
    outgain_grad = jnp.sum(upstream * unit_second, 0)
    outbias_grad = jnp.sum(upstream, 0)
    second_grad = norm_back(upstream, unit_second, scale_second, outgain.astype(jnp.float32))
    branch_grad = second_grad.astype(jnp.bfloat16)
    shrinkbias_grad = column_sum(branch_grad)
    shrinkmap_grad = rows_product(active, branch_grad)
    active_grad = cols_product(branch_grad, shrinkmap)
    unused_value, gelu_pull = jax.vjp(partial(jax.nn.gelu, approximate=False), inner_pre)
    inner_grad = gelu_pull(active_grad)[0].astype(jnp.bfloat16)
    expandbias_grad = column_sum(inner_grad)
    expandmap_grad = rows_product(normed, inner_grad)
    normed_grad = second_grad + cols_product(inner_grad, expandmap)
    normgain_grad = jnp.sum(normed_grad * unit_first, 0)
    normbias_grad = jnp.sum(normed_grad, 0)
    first_grad = norm_back(normed_grad, unit_first, scale_first, normgain.astype(jnp.float32))
    attended_grad = first_grad.astype(jnp.bfloat16)
    mixbias_grad = column_sum(attended_grad)
    mixmap_grad = rows_product(context, attended_grad)
    context_grad = (
        cols_product(attended_grad, mixmap).astype(jnp.bfloat16).reshape(seqrows, qlength, H, HD)
    )
    query_heads = queries.reshape(seqrows, qlength, H, HD)

    def attend_back(operands):
        (
            query_one,
            key_one,
            value_one,
            prior_one,
            same_one,
            total_one,
            upstream_one,
            cotangent_one,
        ) = operands
        scores = jnp.einsum("qhe,khe->hqk", query_one, key_one, preferred_element_type=jnp.float32)
        logits = prior_one.astype(jnp.float32) + scores * factor
        attention = jnp.exp(jnp.where(same_one, logits, mask_fill) - total_one)
        prob_grad = jnp.einsum(
            "qhe,khe->hqk", upstream_one, value_one, preferred_element_type=jnp.float32
        )
        row_dot = jnp.sum(prob_grad * attention, -1, keepdims=True)
        logit_grad = (cotangent_one.astype(jnp.float32) + attention * (prob_grad - row_dot)).astype(
            jnp.bfloat16
        )
        query_part = (
            jnp.einsum("hqk,khe->qhe", logit_grad, key_one, preferred_element_type=jnp.float32)
            * factor
        )
        key_part = (
            jnp.einsum("hqk,qhe->khe", logit_grad, query_one, preferred_element_type=jnp.float32)
            * factor
        )
        value_part = jnp.einsum(
            "hqk,qhe->khe",
            attention.astype(jnp.bfloat16),
            upstream_one,
            preferred_element_type=jnp.float32,
        )
        return (logit_grad, query_part, key_part, value_part)

    logits_grad, query_grad, key_partial, value_partial = lax.map(
        attend_back,
        (
            query_heads,
            key_heads,
            value_heads,
            prev_logits,
            same_segment,
            log_total,
            context_grad,
            logit_cotangent,
        ),
    )
    key_grad, value_grad = (
        lax.psum_scatter(
            key_partial.reshape(seqrows, klength, width).astype(jnp.bfloat16),
            "seq",
            scatter_dimension=1,
            tiled=True,
        ).astype(jnp.float32),
        lax.psum_scatter(
            value_partial.reshape(seqrows, klength, width).astype(jnp.bfloat16),
            "seq",
            scatter_dimension=1,
            tiled=True,
        ).astype(jnp.float32),
    )
    query_grad = query_grad.reshape(seqrows * qlength, width).astype(jnp.bfloat16)
    key_grad = key_grad.reshape(seqrows * qlength, width).astype(jnp.bfloat16)
    value_grad = value_grad.reshape(seqrows * qlength, width).astype(jnp.bfloat16)
    querymap_grad = rows_product(token_rows, query_grad)
    querybias_grad = column_sum(query_grad)
    keymap_grad = rows_product(token_rows, key_grad)
    valuemap_grad = rows_product(token_rows, value_grad)
    valuebias_grad = column_sum(value_grad)
    tokens_grad = (
        first_grad
        + cols_product(query_grad, querymap)
        + cols_product(key_grad, keymap)
        + cols_product(value_grad, valuemap)
    )
    owned = (
        lax.psum_scatter(querymap_grad, ("dp", "seq"), scatter_dimension=0, tiled=True),
        lax.psum_scatter(querybias_grad, ("dp", "seq"), scatter_dimension=0, tiled=True),
        lax.psum_scatter(keymap_grad, ("dp", "seq"), scatter_dimension=0, tiled=True),
        lax.psum_scatter(valuemap_grad, ("dp", "seq"), scatter_dimension=0, tiled=True),
        lax.psum_scatter(valuebias_grad, ("dp", "seq"), scatter_dimension=0, tiled=True),
        lax.psum_scatter(mixmap_grad, ("dp", "seq"), scatter_dimension=0, tiled=True),
        lax.psum_scatter(mixbias_grad, ("dp", "seq"), scatter_dimension=0, tiled=True),
        lax.psum_scatter(normgain_grad, ("dp", "seq"), scatter_dimension=0, tiled=True),
        lax.psum_scatter(normbias_grad, ("dp", "seq"), scatter_dimension=0, tiled=True),
        lax.psum_scatter(expandmap_grad, ("dp", "seq"), scatter_dimension=0, tiled=True),
        lax.psum_scatter(expandbias_grad, ("dp", "seq"), scatter_dimension=0, tiled=True),
        lax.psum_scatter(shrinkmap_grad, ("dp", "seq"), scatter_dimension=0, tiled=True),
        lax.psum_scatter(shrinkbias_grad, ("dp", "seq"), scatter_dimension=0, tiled=True),
        lax.psum_scatter(outgain_grad, ("dp", "seq"), scatter_dimension=0, tiled=True),
        lax.psum_scatter(outbias_grad, ("dp", "seq"), scatter_dimension=0, tiled=True),
    )
    return (
        layer_out.reshape(seqrows, qlength, width).astype(jnp.bfloat16),
        raw_logits,
        tokens_grad.reshape(seqrows, qlength, width).astype(jnp.bfloat16),
        logits_grad,
    ) + tuple(owned)


def solution(mesh):
    in_specs = (
        P("dp", "seq", None),
        P("dp", None, "seq", None),
        P("dp", None),
        P("dp", "seq", None),
        P("dp", None, "seq", None),
        P(("dp", "seq"), None),
        P(("dp", "seq")),
        P(("dp", "seq"), None),
        P(("dp", "seq"), None),
        P(("dp", "seq")),
        P(("dp", "seq"), None),
        P(("dp", "seq")),
        P(("dp", "seq")),
        P(("dp", "seq")),
        P(("dp", "seq"), None),
        P(("dp", "seq")),
        P(("dp", "seq"), None),
        P(("dp", "seq")),
        P(("dp", "seq")),
        P(("dp", "seq")),
    )
    out_specs = (
        P("dp", "seq", None),
        P("dp", None, "seq", None),
        P("dp", "seq", None),
        P("dp", None, "seq", None),
        P(("dp", "seq"), None),
        P(("dp", "seq")),
        P(("dp", "seq"), None),
        P(("dp", "seq"), None),
        P(("dp", "seq")),
        P(("dp", "seq"), None),
        P(("dp", "seq")),
        P(("dp", "seq")),
        P(("dp", "seq")),
        P(("dp", "seq"), None),
        P(("dp", "seq")),
        P(("dp", "seq"), None),
        P(("dp", "seq")),
        P(("dp", "seq")),
        P(("dp", "seq")),
    )
    return jax.shard_map(body, mesh=mesh, in_specs=in_specs, out_specs=out_specs, check_vma=False)
```

profile of v0, /device:TPU:0, one launch (start us, length us, event | category | flops | bytes accessed | tf_op | source)
XLA Modules:
  0.0 1690.0 jit_solution(7666844894113663365)
XLA Ops:
  17.0 42.5 %all-reduce.28 = (bf16[3072]{0:T(1024)(128)(2,1)S(1)}, bf16[768]{0:T(1024)(128)(2,1)S(1)}, bf16[768]{0:T(1024)(128)(2,1)S(1)}, bf16[768]{0:T(1024)(128)(2,1)S(1)...) all-reduce(bf16[3072]{0:T(1024)(128)(2,1)S(1)} %dynamic-update-slic, ...), channel_id=1, replica_groups=mesh['dp'=16,'seq'=2] {'dp','seq'}, use_global_device_ids=true, to_apply=%add.5 | all-reduce | flops 9216 | bytes 36864
  71.7 51.8 %all-gather.19.cloned.1.call-done = bf16[768,768]{1,0:T(8,128)(2,1)} async-done(((bf16[24,768]{1,0:T(8,128)(2,1)}), bf16[768,768]{1,0:T(8,128)(2,1)}) %all-gather.19.cloned.1.call-update) | async-done | bytes 1179664 | tf_op jit(solution)/shard_map/all_gather | solution.py:69
  130.8 48.5 %all-gather.17.cloned.1.call-done = bf16[768,768]{1,0:T(8,128)(2,1)} async-done(((bf16[24,768]{1,0:T(8,128)(2,1)}), bf16[768,768]{1,0:T(8,128)(2,1)}) %all-gather.17.cloned.1.call-update) | async-done | bytes 1179664 | tf_op jit(solution)/shard_map/all_gather | solution.py:67
  214.1 32.1 %while.40 = (s32[]{:T(128)}, bf16[3,12,256,512]{3,2,1,0:T(8,128)(2,1)}, bf16[3,256,12,64]{1,3,2,0:T(8,128)(2,1)}, bf16[3,12,256,512]{3,2,1,0:T(8,128)(2,1)}, bf1...) while((s32[]{:T(128)}, ...), condition=%wide.region_3.4_spmd, body=%wide.region_0.3_spmd.sunk | while | flops 418578944 | bytes 34237024 | solution.py:135
  248.9 14.2 all-gather.27.cloned.1.call-done
  267.5 61.0 %all-gather.29.cloned.1.call-done = bf16[768,3072]{1,0:T(8,128)(2,1)} async-done(((bf16[24,3072]{1,0:T(8,128)(2,1)}), bf16[768,3072]{1,0:T(8,128)(2,1)}) %all-gather.29.cloned.1.call-update) | async-done | bytes 4718608 | tf_op jit(solution)/shard_map/all_gather | solution.py:76
  328.6 64.9 %all-gather.31.cloned.1.call-done = bf16[3072,768]{1,0:T(8,128)(2,1)} async-done(((bf16[96,768]{1,0:T(8,128)(2,1)}), bf16[3072,768]{1,0:T(8,128)(2,1)}) %all-gather.31.cloned.1.call-update) | async-done | bytes 4718608 | tf_op jit(solution)/shard_map/all_gather | solution.py:78
  393.4 31.3 %fusion.143 = (f32[768]{0:T(1024)S(1)}, f32[768,768]{1,0:T(8,128)S(1)}) fusion(f32[768]{0:T(1024)S(1)} %convert_element_type.242, bf16[3072,768]{1,0:T(8,128)(2,1)} %all-gather.31.cloned.1.call-done, bf16[768,3072]{1,0:T(8,128)(2,1)} %all-gather.29.cloned.1.call-done, f32[3072]{0:T(1024)S(1)} %convert_element_type.240, f32[768,768]{1,0:T(8,128)} %copy-done.20, ...), kind=kOutput, calls=%fused_computation.221 | convolution fusion | flops 7411727360 | bytes 14186496 | tf_op jit(solution)/shard_map/dot_general | solution.py:14
  432.6 39.5 %all-reduce.27 = (bf16[768]{0:T(1024)(128)(2,1)S(1)}, bf16[768]{0:T(1024)(128)(2,1)S(1)}, bf16[768]{0:T(1024)(128)(2,1)S(1)}, bf16[768]{0:T(1024)(128)(2,1)S(1)}...) all-reduce(bf16[768]{0:T(1024)(128)(2,1)S(1)} %dynamic-update-slice, ...), channel_id=1, replica_groups=mesh['dp'=16,'seq'=2] {'dp','seq'}, use_global_device_ids=true, to_apply=%add.10 | all-reduce | flops 8448 | bytes 33792
  483.1 52.2 %all-gather.39.cloned.1.call-done = bf16[768,768]{1,0:T(8,128)(2,1)} async-done(((bf16[24,768]{1,0:T(8,128)(2,1)}), bf16[768,768]{1,0:T(8,128)(2,1)}) %all-gather.39.cloned.1.call-update) | async-done | bytes 1179664 | tf_op jit(solution)/shard_map/all_gather | solution.py:69
  543.0 48.1 %all-gather.37.cloned.1.call-done = bf16[768,768]{1,0:T(8,128)(2,1)} async-done(((bf16[24,768]{1,0:T(8,128)(2,1)}), bf16[768,768]{1,0:T(8,128)(2,1)}) %all-gather.37.cloned.1.call-update) | async-done | bytes 1179664 | tf_op jit(solution)/shard_map/all_gather | solution.py:67
  620.1 31.9 %while.41 = (s32[]{:T(128)}, bf16[3,256,12,64]{1,3,2,0:T(8,128)(2,1)}, f32[3,12,256,1]{2,1,3,0:T(8,128)}, bf16[3,512,12,64]{1,3,2,0:T(8,128)(2,1)}, pred[3,1,256...) while((s32[]{:T(128)}, ...), condition=%wide.region_11.12_spmd, body=%wide.region_8.11_spmd.sunk | while | flops 418575360 | bytes 24878176 | solution.py:135
  655.9 18.1 %all-gather.43.cloned.1.call-done = bf16[768,768]{1,0:T(8,128)(2,1)} async-done(((bf16[24,768]{1,0:T(8,128)(2,1)}), bf16[768,768]{1,0:T(8,128)(2,1)}) %all-gather.43.cloned.1.call-update) | async-done | bytes 1179664 | tf_op jit(solution)/shard_map/all_gather | solution.py:72
  679.2 60.1 %all-gather.45.cloned.1.call-done = bf16[768,3072]{1,0:T(8,128)(2,1)} async-done(((bf16[24,3072]{1,0:T(8,128)(2,1)}), bf16[768,3072]{1,0:T(8,128)(2,1)}) %all-gather.45.cloned.1.call-update) | async-done | bytes 4718608 | tf_op jit(solution)/shard_map/all_gather | solution.py:76
  739.3 28.4 %multiply_convert_fusion = (bf16[768,3072]{1,0:T(8,128)(2,1)}, f32[768,3072]{1,0:T(8,128)}, f32[768,3072]{1,0:T(8,128)}) fusion(f32[3072]{0:T(1024)S(1)} %copy-done.38, bf16[768,3072]{1,0:T(8,128)(2,1)} %all-gather.45.cloned.1.call-done, f32[768,768]{1,0:T(8,128)} %copy-done.6, f32[768]{0:T(1024)S(1)} %convert_element_type.255, ...), kind=kOutput, calls=%fused_computation.89 | convolution fusion | flops 3782541312 | bytes 30695424 | tf_op jit(solution)/shard_map/dot_general | solution.py:14
  767.6 36.4 %all-gather.47.cloned.1.call-done = bf16[3072,768]{1,0:T(8,128)(2,1)} async-done(((bf16[96,768]{1,0:T(8,128)(2,1)}), bf16[3072,768]{1,0:T(8,128)(2,1)}) %all-gather.47.cloned.1.call-update) | async-done | bytes 4718608 | tf_op jit(solution)/shard_map/all_gather | solution.py:78
  855.3 101.8 %while.42 = (s32[]{:T(128)}, bf16[3,12,256,512]{3,2,1,0:T(8,128)(2,1)}, bf16[3,256,12,64]{1,3,2,0:T(8,128)(2,1)}, bf16[3,512,12,64]{1,3,2,0:T(8,128)(2,1)}, bf16...) while((s32[]{:T(128)}, ...), condition=%wide.region_22.23_spmd, body=%wide.region_20.22_spmd.sunk | while | flops 1026100736 | bytes 124696864 | solution.py:315
  1009.9 41.7 %all-reduce.26 = (f32[768]{0:T(1024)S(1)}, f32[768]{0:T(1024)S(1)}, f32[768]{0:T(1024)S(1)}, f32[768]{0:T(1024)S(1)}, f32[768]{0:T(1024)S(1)}, /*index=5*/f32[30...) all-reduce(f32[768]{0:T(1024)S(1)} %reduce_sum.231, ...), channel_id=5, replica_groups=mesh['dp'=16,'seq'=2] {'dp','seq'}, use_global_device_ids=true, to_apply=%region_27.28.clone | all-reduce | flops 9216 | bytes 73728
  1063.6 22.2 %reduce-scatter.19.cloned.1.call-done = f32[24,768]{1,0:T(8,128)} async-done(((f32[768,768]{1,0:T(8,128)}), f32[24,768]{1,0:T(8,128)}) %reduce-scatter.19.cloned.1.call-update) | async-done | bytes 73744 | tf_op jit(solution)/shard_map/reduce_scatter | solution.py:362
  1085.8 104.4 %reduce-scatter.25.cloned.1.call-done = f32[24,768]{1,0:T(8,128)} async-done(((f32[768,768]{1,0:T(8,128)}), f32[24,768]{1,0:T(8,128)}) %reduce-scatter.25.cloned.1.call-update) | async-done | bytes 73744
  1190.2 104.5 %reduce-scatter.27.cloned.1.call-done = f32[24,768]{1,0:T(8,128)} async-done(((f32[768,768]{1,0:T(8,128)}), f32[24,768]{1,0:T(8,128)}) %reduce-scatter.27.cloned.1.call-update) | async-done | bytes 73744
  1294.7 104.5 %reduce-scatter.29.cloned.1.call-done = f32[24,768]{1,0:T(8,128)} async-done(((f32[768,768]{1,0:T(8,128)}), f32[24,768]{1,0:T(8,128)}) %reduce-scatter.29.cloned.1.call-update) | async-done | bytes 73744
  1399.3 142.0 %reduce-scatter.23.cloned.1.call-done = f32[96,768]{1,0:T(8,128)} async-done(((f32[3072,768]{1,0:T(8,128)}), f32[96,768]{1,0:T(8,128)}) %reduce-scatter.23.cloned.1.call-update) | async-done | bytes 294928 | tf_op jit(solution)/shard_map/reduce_scatter | solution.py:368
  1541.2 141.7 %reduce-scatter.21.cloned.1.call-done = f32[24,3072]{1,0:T(8,128)} async-done(((f32[768,3072]{1,0:T(8,128)}), f32[24,3072]{1,0:T(8,128)}) %reduce-scatter.21.cloned.1.call-update) | async-done | bytes 294928 | tf_op jit(solution)/shard_map/reduce_scatter | solution.py:366
  (367 shorter events, 416.4 us)
Async XLA Ops:
  7.2 60.6 %all-gather.23.cloned.1.call-start = ((), (), s32[]{:S(2)}) async-start(), calls=%async_computation.11 | async-start | bytes 1216512 | tf_op jit(solution)/shard_map/all_gather | solution.py:70
  7.9 115.6 %all-gather.19.cloned.1.call-start = ((), (), s32[]{:S(2)}) async-start(), calls=%async_computation.9 | async-start | bytes 1216512 | tf_op jit(solution)/shard_map/all_gather | solution.py:69
  8.7 170.6 %all-gather.17.cloned.1.call-start = ((), (), s32[]{:S(2)}) async-start(), calls=%async_computation.8 | async-start | bytes 1216512 | tf_op jit(solution)/shard_map/all_gather | solution.py:67
  9.4 181.7 %all-gather.25.cloned.1.call-start = ((), (), s32[]{:S(2)}) async-start(), calls=%async_computation.12 | async-start | bytes 3538944 | tf_op jit(solution)/shard_map/all_gather | solution.py:111
  71.7 133.6 %all-gather.21.cloned.1.call-start = ((), (), s32[]{:S(2)}) async-start(), calls=%async_computation.10 | async-start | bytes 3538944 | tf_op jit(solution)/shard_map/all_gather | solution.py:110
  126.9 136.2 %all-gather.27.cloned.1.call-start = ((), (), s32[]{:S(2)}) async-start(), calls=%async_computation.13 | async-start | bytes 1216512 | tf_op jit(solution)/shard_map/all_gather | solution.py:72
  127.5 201.1 %all-gather.29.cloned.1.call-start = ((), (), s32[]{:S(2)}) async-start(), calls=%async_computation.14 | async-start | bytes 4866048 | tf_op jit(solution)/shard_map/all_gather | solution.py:76
  128.2 265.2 %all-gather.31.cloned.1.call-start = ((), (), s32[]{:S(2)}) async-start(), calls=%async_computation.15 | async-start | bytes 4866048 | tf_op jit(solution)/shard_map/all_gather | solution.py:78
  129.0 350.7 %all-gather.33.cloned.1.call-start = ((), (), s32[]{:S(2)}) async-start(), calls=%async_computation.16 | async-start | bytes 1216512 | tf_op jit(solution)/shard_map/all_gather | solution.py:70
  426.9 108.4 %all-gather.39.cloned.1.call-start = ((), (), s32[]{:S(2)}) async-start(), calls=%async_computation.19 | async-start | bytes 1216512 | tf_op jit(solution)/shard_map/all_gather | solution.py:69
  427.5 163.5 %all-gather.37.cloned.1.call-start = ((), (), s32[]{:S(2)}) async-start(), calls=%async_computation.18 | async-start | bytes 1216512 | tf_op jit(solution)/shard_map/all_gather | solution.py:67
  428.3 174.1 %all-gather.35.cloned.1.call-start = ((), (), s32[]{:S(2)}) async-start(), calls=%async_computation.17 | async-start | bytes 3538944 | tf_op jit(solution)/shard_map/all_gather | solution.py:111
  483.1 133.0 %all-gather.41.cloned.1.call-start = ((), (), s32[]{:S(2)}) async-start(), calls=%async_computation.20 | async-start | bytes 3538944 | tf_op jit(solution)/shard_map/all_gather | solution.py:110
  538.7 135.2 %all-gather.43.cloned.1.call-start = ((), (), s32[]{:S(2)}) async-start(), calls=%async_computation.21 | async-start | bytes 1216512 | tf_op jit(solution)/shard_map/all_gather | solution.py:72
  539.3 199.9 %all-gather.45.cloned.1.call-start = ((), (), s32[]{:S(2)}) async-start(), calls=%async_computation.22 | async-start | bytes 4866048 | tf_op jit(solution)/shard_map/all_gather | solution.py:76
  539.9 264.1 %all-gather.47.cloned.1.call-start = ((), (), s32[]{:S(2)}) async-start(), calls=%async_computation.23 | async-start | bytes 4866048 | tf_op jit(solution)/shard_map/all_gather | solution.py:78
  542.9 425.5 %reduce-scatter.15.cloned.1.call-start = ((), (), s32[]{:S(2)}) async-start(), calls=%async_computation.24 | async-start | bytes 3538944 | tf_op jit(solution)/shard_map/reduce_scatter | solution.py:329
  957.1 21.7 %reduce-scatter.17.cloned.1.call-start = ((), (), s32[]{:S(2)}) async-start(), calls=%async_computation.25 | async-start | bytes 3538944 | tf_op jit(solution)/shard_map/reduce_scatter | solution.py:335
  957.7 128.1 %reduce-scatter.19.cloned.1.call-start = ((), (), s32[]{:S(2)}) async-start(), calls=%async_computation.26 | async-start | bytes 2433024 | tf_op jit(solution)/shard_map/reduce_scatter | solution.py:362
  961.6 228.6 %reduce-scatter.25.cloned.1.call-start = ((), (), s32[]{:S(2)}) async-start(), calls=%async_computation.29 | async-start | bytes 2433024
  968.4 326.4 %reduce-scatter.27.cloned.1.call-start = ((), (), s32[]{:S(2)}) async-start(), calls=%async_computation.30 | async-start | bytes 2433024
  973.2 426.1 %reduce-scatter.29.cloned.1.call-start = ((), (), s32[]{:S(2)}) async-start(), calls=%async_computation.31 | async-start | bytes 2433024
  983.6 557.6 %reduce-scatter.23.cloned.1.call-start = ((), (), s32[]{:S(2)}) async-start(), calls=%async_computation.28 | async-start | bytes 9732096 | tf_op jit(solution)/shard_map/reduce_scatter | solution.py:368
  994.2 688.8 %reduce-scatter.21.cloned.1.call-start = ((), (), s32[]{:S(2)}) async-start(), calls=%async_computation.27 | async-start | bytes 9732096 | tf_op jit(solution)/shard_map/reduce_scatter | solution.py:366
  (62 other events, 1012.8 us)
Sparse Core Ops, SparseCore 0:
  10.9 56.8 all-gather.22
  70.7 52.7 all-gather.18
  126.4 52.8 all-gather.16
  181.2 9.8 all-gather.24
  193.1 12.1 all-gather.20
  208.0 55.0 all-gather.26
  266.0 62.4 all-gather.28
  331.5 61.9 all-gather.30
  427.1 52.5 all-gather.32
  482.4 52.8 all-gather.38
  538.2 52.8 all-gather.36
  592.5 9.8 all-gather.34
  603.9 12.1 all-gather.40
  618.8 55.1 all-gather.42
  676.7 62.4 all-gather.44
  742.0 61.9 all-gather.46
  957.2 8.2 reduce-scatter.14
  967.6 11.1 reduce-scatter.16
  984.7 101.0 reduce-scatter.18
  1091.5 98.6 reduce-scatter.24
  1196.1 98.6 reduce-scatter.26
  1300.6 98.6 reduce-scatter.28
  1405.7 135.4 reduce-scatter.22
  1547.5 135.3 reduce-scatter.20
where the time goes:
time: 1700 us; the launch traced here: 1690 us
  waiting for transfers between devices  1130 us (66%)
  matrix products  260 us (15%)
  blocking collectives  124 us (7%)
  local copies, waits for them, and re-layouts  102 us (6%)
  other arithmetic  62.3 us (4%)
    unnamed x27, waiting for transfers between devices  320 us
    reduce_scatter x1, waiting for transfers between devices, body(): lax.psum_scatter(shrinkmap_grad, ('dp', 'seq'), scatter_dimension=0, tile...  142 us
    reduce_scatter x1, waiting for transfers between devices, body(): lax.psum_scatter(expandmap_grad, ('dp', 'seq'), scatter_dimension=0, tile...  142 us
    unnamed x3, blocking collectives  124 us
    all_gather x2, waiting for transfers between devices, forward(): lax.all_gather(expandmap, ('dp', 'seq'), axis=0, tiled=True)  121 us
    all_gather x2, waiting for transfers between devices, forward(): lax.all_gather(keymap, ('dp', 'seq'), axis=0, tiled=True)  104 us
    all_gather x2, waiting for transfers between devices, forward(): lax.all_gather(shrinkmap, ('dp', 'seq'), axis=0, tiled=True)  101 us
    all_gather x2, waiting for transfers between devices, forward(): lax.all_gather(querymap, ('dp', 'seq'), axis=0, tiled=True)  96.6 us
  transfers between devices with their start and end apart: 24, of which 23 were waited for; matrix products, arithmetic and copies ran while one was open for 13% of the time, Pallas kernels for 0%

commit v1 on v0

--- a/solution.py
+++ b/solution.py
@@ -63,6 +63,21 @@
         outgain,
         outbias,
     ) = shards
+
+    def register_vector(own_rows, ndim_at):
+        left_arr = jax.lax.axis_size(("dp", "seq"))
+        m_next, carry_out = (left_arr, jax.lax.axis_index(("dp", "seq")))
+        ready, main = (own_rows, 1)
+        while main < m_next:
+            answer = jax.lax.ppermute(
+                ready, ("dp", "seq"), perm=[(q, q ^ main) for q in range(m_next)]
+            )
+            tile_out = jnp.concatenate([ready, answer], axis=ndim_at)
+            w2 = jnp.concatenate([answer, ready], axis=ndim_at)
+            ready = jnp.where(carry_out & main == 0, tile_out, w2)
+            main = 2 * main
+        return ready
+
     weights = (
         lax.all_gather(querymap, ("dp", "seq"), axis=0, tiled=True),
         lax.all_gather(querybias, ("dp", "seq"), axis=0, tiled=True),
@@ -73,7 +88,7 @@
         lax.all_gather(mixbias, ("dp", "seq"), axis=0, tiled=True),
         lax.all_gather(normgain, ("dp", "seq"), axis=0, tiled=True),
         lax.all_gather(normbias, ("dp", "seq"), axis=0, tiled=True),
-        lax.all_gather(expandmap, ("dp", "seq"), axis=0, tiled=True),
+        register_vector(expandmap, ndim_at=0),
         lax.all_gather(expandbias, ("dp", "seq"), axis=0, tiled=True),
         lax.all_gather(shrinkmap, ("dp", "seq"), axis=0, tiled=True),
         lax.all_gather(shrinkbias, ("dp", "seq"), axis=0, tiled=True),

time: 1700 us -> 1640 us (0.965)
  waiting for transfers between devices: 1130 us -> 1040 us
    all_gather x2 -> x0, waiting for transfers between devices: 121 us -> none  [forward(): lax.all_gather(expandmap, ('dp', 'seq'), axis=0, tiled=True)]
    all_gather x2, waiting for transfers between devices: 96.6 us -> 0.01 us  [forward(): lax.all_gather(querymap, ('dp', 'seq'), axis=0, tiled=True)]
    ppermute x0 -> x10, waiting for transfers between devices: none -> 96.2 us  [register_vector(): jax.lax.ppermute(ready, ('dp', 'seq'), perm=[(q, q ^ main) for q in range...]
    all_gather x2, waiting for transfers between devices: 32.3 us -> 123 us  [forward(): lax.all_gather(mixmap, ('dp', 'seq'), axis=0, tiled=True)]
    all_gather x2, waiting for transfers between devices: 101 us -> 65 us  [forward(): lax.all_gather(shrinkmap, ('dp', 'seq'), axis=0, tiled=True)]
    dot_general x11 -> x12, matrix products: 93.1 us -> 99.6 us  [matmul(): return jnp.dot(left_side, right_side, preferred_element_type=jnp.float32)]
    unnamed x27 -> x25, waiting for transfers between devices: 320 us -> 317 us
    unnamed x143 -> x157, local copies, waits for them, and re-layouts: 37.7 us -> 34.8 us
  transfers between devices with their start and end apart: 24 -> 32, of which waited for: 23 -> 25; matrix products, arithmetic and copies ran while one was open for 13% -> 16% of each run, Pallas kernels for 0% -> 0%
where the time goes in v1:
time: 1640 us; the launch traced here: 1630 us
  waiting for transfers between devices  1040 us (63%)
  matrix products  268 us (16%)
  blocking collectives  124 us (8%)
  local copies, waits for them, and re-layouts  99.1 us (6%)
  other arithmetic  71.5 us (4%)
    unnamed x25, waiting for transfers between devices  317 us
    reduce_scatter x1, waiting for transfers between devices, body(): lax.psum_scatter(shrinkmap_grad, ('dp', 'seq'), scatter_dimension=0, tile...  142 us
    reduce_scatter x1, waiting for transfers between devices, body(): lax.psum_scatter(expandmap_grad, ('dp', 'seq'), scatter_dimension=0, tile...  142 us
    unnamed x3, blocking collectives  124 us
    all_gather x2, waiting for transfers between devices, forward(): lax.all_gather(mixmap, ('dp', 'seq'), axis=0, tiled=True)  123 us
    all_gather x2, waiting for transfers between devices, forward(): lax.all_gather(keymap, ('dp', 'seq'), axis=0, tiled=True)  104 us
    dot_general x12, matrix products, matmul(): return jnp.dot(left_side, right_side, preferred_element_type=jnp.float32)  99.6 us
    ppermute x10, waiting for transfers between devices, register_vector(): jax.lax.ppermute(ready, ('dp', 'seq'), perm=[(q, q ^ main) for q in range...  96.2 us
  transfers between devices with their start and end apart: 32, of which 25 were waited for; matrix products, arithmetic and copies ran while one was open for 16% of the time, Pallas kernels for 0%

profile of v1, /device:TPU:0, one launch (start us, length us, event | category | flops | bytes accessed | tf_op | source)
XLA Modules:
  0.0 1630.1 jit_solution(7687420342198875384)
XLA Ops:
  17.0 42.5 %all-reduce.28 = (bf16[3072]{0:T(1024)(128)(2,1)S(1)}, bf16[768]{0:T(1024)(128)(2,1)S(1)}, bf16[768]{0:T(1024)(128)(2,1)S(1)}, bf16[768]{0:T(1024)(128)(2,1)S(1)...) all-reduce(bf16[3072]{0:T(1024)(128)(2,1)S(1)} %dynamic-update-slic, ...), channel_id=1, replica_groups=mesh['dp'=16,'seq'=2] {'dp','seq'}, use_global_device_ids=true, to_apply=%add.5 | all-reduce | flops 9216 | bytes 36864
  71.7 51.8 %all-gather.17.cloned.1.call-done = bf16[768,768]{1,0:T(8,128)(2,1)} async-done(((bf16[24,768]{1,0:T(8,128)(2,1)}), bf16[768,768]{1,0:T(8,128)(2,1)}) %all-gather.17.cloned.1.call-update) | async-done | bytes 1179664 | tf_op jit(solution)/shard_map/all_gather | solution.py:84
  139.6 13.6 collective-permute-done.2
  156.0 27.6 %collective-permute-done.3 = bf16[192,3072]{1,0:T(8,128)(2,1)S(1)} collective-permute-done((bf16[192,3072]{1,0:T(8,128)(2,1)S(1)}, bf16[192,3072]{1,0:T(8,128)(2,1)S(1)}, u32[]{:S(2)}, u32[]{:S(2)}) %collective-permute-start.3) | collective-permute-done | bytes 1179680 | tf_op jit(solution)/shard_map/ppermute | solution.py:72
  214.5 32.1 %while.40 = (s32[]{:T(128)}, bf16[3,12,256,512]{3,2,1,0:T(8,128)(2,1)}, bf16[3,256,12,64]{1,3,2,0:T(8,128)(2,1)}, bf16[3,12,256,512]{3,2,1,0:T(8,128)(2,1)}, bf1...) while((s32[]{:T(128)}, ...), condition=%wide.region_3.4_spmd, body=%wide.region_0.3_spmd.sunk | while | flops 418578944 | bytes 34237024 | solution.py:150
  250.3 58.6 %all-gather.25.cloned.1.call-done = bf16[768,768]{1,0:T(8,128)(2,1)} async-done(((bf16[24,768]{1,0:T(8,128)(2,1)}), bf16[768,768]{1,0:T(8,128)(2,1)}) %all-gather.25.cloned.1.call-update) | async-done | bytes 1179664 | tf_op jit(solution)/shard_map/all_gather | solution.py:87
  312.6 27.4 %fusion.69.clone.3.clone.4 = bf16[768,3072]{1,0:T(8,128)(2,1)} fusion(bf16[384,3072]{1,0:T(8,128)(2,1)} %collective-permute-done.4, bf16[384,3072]{1,0:T(8,128)(2,1)} %maximum_select_fusion.5, f32[3072]{0:T(1024)S(1)} %convert_element_type.240, pred[]{:T(512)S(6)} %eq.43, f32[768,768]{1,0:T(8,128)S(1)} %get-tuple-element.516, ...), kind=kOutput, calls=%fused_computation.85.clone.clone.clone.clone.clone.clone.clone.1 | convolution fusion | flops 3803774976 | bytes 11821057 | tf_op jit(solution)/shard_map/dot_general | solution.py:14
  340.1 34.3 %all-gather.27.cloned.1.call-done = bf16[3072,768]{1,0:T(8,128)(2,1)} async-done(((bf16[96,768]{1,0:T(8,128)(2,1)}), bf16[3072,768]{1,0:T(8,128)(2,1)}) %all-gather.27.cloned.1.call-update) | async-done | bytes 4718608 | tf_op jit(solution)/shard_map/all_gather | solution.py:93
  387.6 39.7 %all-reduce.27 = (bf16[768]{0:T(1024)(128)(2,1)}, bf16[768]{0:T(1024)(128)(2,1)S(1)}, bf16[768]{0:T(1024)(128)(2,1)}, bf16[768]{0:T(1024)(128)(2,1)}, bf16[768]{...) all-reduce(bf16[768]{0:T(1024)(128)(2,1)S(1)} %dynamic-update-slice, ...), channel_id=1, replica_groups=mesh['dp'=16,'seq'=2] {'dp','seq'}, use_global_device_ids=true, to_apply=%add.10 | all-reduce | flops 8448 | bytes 33792
  439.8 52.3 %all-gather.35.cloned.1.call-done = bf16[768,768]{1,0:T(8,128)(2,1)} async-done(((bf16[24,768]{1,0:T(8,128)(2,1)}), bf16[768,768]{1,0:T(8,128)(2,1)}) %all-gather.35.cloned.1.call-update) | async-done | bytes 1179664 | tf_op jit(solution)/shard_map/all_gather | solution.py:84
  508.2 13.7 collective-permute-done.7
  529.1 23.2 %collective-permute-done.8 = bf16[192,3072]{1,0:T(8,128)(2,1)S(1)} collective-permute-done((bf16[192,3072]{1,0:T(8,128)(2,1)S(1)}, bf16[192,3072]{1,0:T(8,128)(2,1)S(1)}, u32[]{:S(2)}, u32[]{:S(2)}) %collective-permute-start.8) | collective-permute-done | bytes 1179680 | tf_op jit(solution)/shard_map/ppermute | solution.py:72
  577.1 31.9 %while.41 = (s32[]{:T(128)}, bf16[3,256,12,64]{1,3,2,0:T(8,128)(2,1)}, f32[3,12,256,1]{2,1,3,0:T(8,128)}, bf16[3,512,12,64]{1,3,2,0:T(8,128)(2,1)}, pred[3,1,256...) while((s32[]{:T(128)}, ...), condition=%wide.region_11.12_spmd, body=%wide.region_8.11_spmd.sunk | while | flops 418575360 | bytes 24878176 | solution.py:150
  613.0 64.8 %all-gather.39.cloned.1.call-done = bf16[768,768]{1,0:T(8,128)(2,1)} async-done(((bf16[24,768]{1,0:T(8,128)(2,1)}), bf16[768,768]{1,0:T(8,128)(2,1)}) %all-gather.39.cloned.1.call-update) | async-done | bytes 1179664 | tf_op jit(solution)/shard_map/all_gather | solution.py:87
  682.5 29.9 %multiply_convert_fusion = (bf16[768,3072]{1,0:T(8,128)(2,1)}, f32[768,3072]{1,0:T(8,128)}, f32[768,3072]{1,0:T(8,128)}) fusion(f32[3072]{0:T(1024)S(1)} %copy-done.39, bf16[384,3072]{1,0:T(8,128)(2,1)} %collective-permute-done.9, bf16[384,3072]{1,0:T(8,128)(2,1)} %maximum_select_fusion.6, pred[]{:T(512)S(6)} %eq.43, ...), kind=kOutput, calls=%fused_computation.89 | convolution fusion | flops 3803774976 | bytes 30695424 | tf_op jit(solution)/shard_map/dot_general | solution.py:14
  712.4 30.7 %all-gather.41.cloned.1.call-done = bf16[3072,768]{1,0:T(8,128)(2,1)} async-done(((bf16[96,768]{1,0:T(8,128)(2,1)}), bf16[3072,768]{1,0:T(8,128)(2,1)}) %all-gather.41.cloned.1.call-update) | async-done | bytes 4718608 | tf_op jit(solution)/shard_map/all_gather | solution.py:93
  796.2 101.8 %while.42 = (s32[]{:T(128)}, bf16[3,12,256,512]{3,2,1,0:T(8,128)(2,1)}, bf16[3,256,12,64]{1,3,2,0:T(8,128)(2,1)}, bf16[3,512,12,64]{1,3,2,0:T(8,128)(2,1)}, bf16...) while((s32[]{:T(128)}, ...), condition=%wide.region_22.23_spmd, body=%wide.region_20.22_spmd.sunk | while | flops 1026100736 | bytes 124696864 | solution.py:330
  950.7 41.7 %all-reduce.26 = (f32[768]{0:T(1024)S(1)}, f32[768]{0:T(1024)S(1)}, f32[768]{0:T(1024)S(1)}, f32[768]{0:T(1024)S(1)}, f32[768]{0:T(1024)S(1)}, /*index=5*/f32[30...) all-reduce(f32[768]{0:T(1024)S(1)} %reduce_sum.231, ...), channel_id=5, replica_groups=mesh['dp'=16,'seq'=2] {'dp','seq'}, use_global_device_ids=true, to_apply=%region_27.28.clone | all-reduce | flops 9216 | bytes 73728
  1004.4 22.0 %reduce-scatter.19.cloned.1.call-done = f32[24,768]{1,0:T(8,128)} async-done(((f32[768,768]{1,0:T(8,128)}), f32[24,768]{1,0:T(8,128)}) %reduce-scatter.19.cloned.1.call-update) | async-done | bytes 73744 | tf_op jit(solution)/shard_map/reduce_scatter | solution.py:377
  1026.5 104.3 %reduce-scatter.25.cloned.1.call-done = f32[24,768]{1,0:T(8,128)} async-done(((f32[768,768]{1,0:T(8,128)}), f32[24,768]{1,0:T(8,128)}) %reduce-scatter.25.cloned.1.call-update) | async-done | bytes 73744
  1130.8 104.5 %reduce-scatter.27.cloned.1.call-done = f32[24,768]{1,0:T(8,128)} async-done(((f32[768,768]{1,0:T(8,128)}), f32[24,768]{1,0:T(8,128)}) %reduce-scatter.27.cloned.1.call-update) | async-done | bytes 73744
  1235.3 104.4 %reduce-scatter.29.cloned.1.call-done = f32[24,768]{1,0:T(8,128)} async-done(((f32[768,768]{1,0:T(8,128)}), f32[24,768]{1,0:T(8,128)}) %reduce-scatter.29.cloned.1.call-update) | async-done | bytes 73744
  1339.7 141.7 %reduce-scatter.23.cloned.1.call-done = f32[96,768]{1,0:T(8,128)} async-done(((f32[3072,768]{1,0:T(8,128)}), f32[96,768]{1,0:T(8,128)}) %reduce-scatter.23.cloned.1.call-update) | async-done | bytes 294928 | tf_op jit(solution)/shard_map/reduce_scatter | solution.py:383
  1481.4 141.6 %reduce-scatter.21.cloned.1.call-done = f32[24,3072]{1,0:T(8,128)} async-done(((f32[768,3072]{1,0:T(8,128)}), f32[24,3072]{1,0:T(8,128)}) %reduce-scatter.21.cloned.1.call-update) | async-done | bytes 294928 | tf_op jit(solution)/shard_map/reduce_scatter | solution.py:381
  (404 shorter events, 444.1 us)
Async XLA Ops:
  7.2 60.6 %all-gather.21.cloned.1.call-start = ((), (), s32[]{:S(2)}) async-start(), calls=%async_computation.11 | async-start | bytes 1216512 | tf_op jit(solution)/shard_map/all_gather | solution.py:85
  7.9 115.6 %all-gather.17.cloned.1.call-start = ((), (), s32[]{:S(2)}) async-start(), calls=%async_computation.9 | async-start | bytes 1216512 | tf_op jit(solution)/shard_map/all_gather | solution.py:84
  8.7 177.9 %all-gather.15.cloned.1.call-start = ((), (), s32[]{:S(2)}) async-start(), calls=%async_computation.8 | async-start | bytes 1216512 | tf_op jit(solution)/shard_map/all_gather | solution.py:82
  9.4 187.9 %all-gather.23.cloned.1.call-start = ((), (), s32[]{:S(2)}) async-start(), calls=%async_computation.12 | async-start | bytes 3538944 | tf_op jit(solution)/shard_map/all_gather | solution.py:126
  71.7 134.0 %all-gather.19.cloned.1.call-start = ((), (), s32[]{:S(2)}) async-start(), calls=%async_computation.10 | async-start | bytes 3538944 | tf_op jit(solution)/shard_map/all_gather | solution.py:125
  126.9 182.0 %all-gather.25.cloned.1.call-start = ((), (), s32[]{:S(2)}) async-start(), calls=%async_computation.13 | async-start | bytes 1216512 | tf_op jit(solution)/shard_map/all_gather | solution.py:87
  130.0 244.3 %all-gather.27.cloned.1.call-start = ((), (), s32[]{:S(2)}) async-start(), calls=%async_computation.14 | async-start | bytes 4866048 | tf_op jit(solution)/shard_map/all_gather | solution.py:93
  153.6 282.6 %all-gather.29.cloned.1.call-start = ((), (), s32[]{:S(2)}) async-start(), calls=%async_computation.15 | async-start | bytes 1216512 | tf_op jit(solution)/shard_map/all_gather | solution.py:85
  185.5 127.1 %collective-permute-start.4 = (bf16[384,3072]{1,0:T(8,128)(2,1)}, bf16[384,3072]{1,0:T(8,128)(2,1)}, u32[]{:S(2)}, u32[]{:S(2)}) collective-permute-start(bf16[384,3072]{1,0:T(8,128)(2,1)} %maximum_select_fusion.5), channel_id=1, source_target_pairs={{0,16},{1,17},{2,18},{3,19},{4,20},{5,21},{6,22},{7,23},{8,24},{9,... | collective-permute-start | bytes 7077896 | tf_op jit(solution)/shard_map/ppermute | solution.py:72
  383.9 108.2 %all-gather.35.cloned.1.call-start = ((), (), s32[]{:S(2)}) async-start(), calls=%async_computation.18 | async-start | bytes 1216512 | tf_op jit(solution)/shard_map/all_gather | solution.py:84
  384.6 170.6 %all-gather.33.cloned.1.call-start = ((), (), s32[]{:S(2)}) async-start(), calls=%async_computation.17 | async-start | bytes 1216512 | tf_op jit(solution)/shard_map/all_gather | solution.py:82
  385.2 180.0 %all-gather.31.cloned.1.call-start = ((), (), s32[]{:S(2)}) async-start(), calls=%async_computation.16 | async-start | bytes 3538944 | tf_op jit(solution)/shard_map/all_gather | solution.py:126
  439.7 133.4 %all-gather.37.cloned.1.call-start = ((), (), s32[]{:S(2)}) async-start(), calls=%async_computation.19 | async-start | bytes 3538944 | tf_op jit(solution)/shard_map/all_gather | solution.py:125
  495.5 182.3 %all-gather.39.cloned.1.call-start = ((), (), s32[]{:S(2)}) async-start(), calls=%async_computation.20 | async-start | bytes 1216512 | tf_op jit(solution)/shard_map/all_gather | solution.py:87
  498.6 244.4 %all-gather.41.cloned.1.call-start = ((), (), s32[]{:S(2)}) async-start(), calls=%async_computation.21 | async-start | bytes 4866048 | tf_op jit(solution)/shard_map/all_gather | solution.py:93
  522.1 30.2 %collective-permute-start.8 = (bf16[192,3072]{1,0:T(8,128)(2,1)S(1)}, bf16[192,3072]{1,0:T(8,128)(2,1)S(1)}, u32[]{:S(2)}, u32[]{:S(2)}) collective-permute-start(bf16[192,3072]{1,0:T(8,128)(2,1)S(1)} %maximum_select_fusion.10), channel_id=1, source_target_pairs={{0,8},{1,9},{2,10},{3,11},{4,12},{5,13},{6,14},{7,15},{8,0},{9,1},... | collective-permute-start | bytes 3538952 | tf_op jit(solution)/shard_map/ppermute | solution.py:72
  529.1 380.5 %reduce-scatter.15.cloned.1.call-start = ((), (), s32[]{:S(2)}) async-start(), calls=%async_computation.22 | async-start | bytes 3538944 | tf_op jit(solution)/shard_map/reduce_scatter | solution.py:344
  554.4 127.0 %collective-permute-start.9 = (bf16[384,3072]{1,0:T(8,128)(2,1)}, bf16[384,3072]{1,0:T(8,128)(2,1)}, u32[]{:S(2)}, u32[]{:S(2)}) collective-permute-start(bf16[384,3072]{1,0:T(8,128)(2,1)} %maximum_select_fusion.6), channel_id=1, source_target_pairs={{0,16},{1,17},{2,18},{3,19},{4,20},{5,21},{6,22},{7,23},{8,24},{9,... | collective-permute-start | bytes 7077896 | tf_op jit(solution)/shard_map/ppermute | solution.py:72
  898.6 127.9 %reduce-scatter.19.cloned.1.call-start = ((), (), s32[]{:S(2)}) async-start(), calls=%async_computation.24 | async-start | bytes 2433024 | tf_op jit(solution)/shard_map/reduce_scatter | solution.py:377
  902.5 228.3 %reduce-scatter.25.cloned.1.call-start = ((), (), s32[]{:S(2)}) async-start(), calls=%async_computation.27 | async-start | bytes 2433024
  909.3 326.0 %reduce-scatter.27.cloned.1.call-start = ((), (), s32[]{:S(2)}) async-start(), calls=%async_computation.28 | async-start | bytes 2433024
  914.3 425.4 %reduce-scatter.29.cloned.1.call-start = ((), (), s32[]{:S(2)}) async-start(), calls=%async_computation.29 | async-start | bytes 2433024
  924.5 556.9 %reduce-scatter.23.cloned.1.call-start = ((), (), s32[]{:S(2)}) async-start(), calls=%async_computation.26 | async-start | bytes 9732096 | tf_op jit(solution)/shard_map/reduce_scatter | solution.py:383
  935.0 688.1 %reduce-scatter.21.cloned.1.call-start = ((), (), s32[]{:S(2)}) async-start(), calls=%async_computation.25 | async-start | bytes 9732096 | tf_op jit(solution)/shard_map/reduce_scatter | solution.py:381
  (77 other events, 1137.5 us)
Sparse Core Ops, SparseCore 0:
  10.9 56.8 all-gather.20
  70.7 52.7 all-gather.16
  126.4 53.2 all-gather.14
  181.7 9.7 all-gather.22
  193.5 12.1 all-gather.18
  208.4 100.4 all-gather.24
  311.8 62.5 all-gather.26
  384.0 52.1 all-gather.28
  439.1 52.8 all-gather.34
  494.8 53.3 all-gather.32
  549.7 9.7 all-gather.30
  560.9 12.1 all-gather.36
  576.0 101.7 all-gather.38
  680.5 62.4 all-gather.40
  898.1 8.2 reduce-scatter.14
  908.5 11.2 reduce-scatter.16
  925.5 100.9 reduce-scatter.18
  1032.2 98.5 reduce-scatter.24
  1136.7 98.5 reduce-scatter.26
  1241.0 98.6 reduce-scatter.28
  1346.1 135.2 reduce-scatter.22
  1487.9 135.1 reduce-scatter.20
